TPU v7x, 256 devices: a whole 4x4x8 slice. The times are simulated.
256 devices in a mesh: expert: 64 (over y_hi, x, z), half: 2 (over y_lo), dp: 2 (over core).
Axes of the slice: x: 4, y: 4 (y_hi: 2, y_lo: 2; y = y_hi * 2 + y_lo), z: 8, core: 2. Of those that a mesh axis runs over, the one named last changes fastest.
Arguments:
- tokens: bfloat16 [16384, 4096], P(('expert', 'dp'), 'half'), may hold values from -6 to 6
- cotangent: bfloat16 [16384, 4096], P(('expert', 'dp'), 'half'), may hold values from -12 to 12
- expert_ids: int32 [16384, 8], P(('expert', 'dp')), may hold values from 0 to 63, as said below
- slot_ids: int32 [16384, 8], P(('expert', 'dp')), may hold values from 0 to 17, as said below
- gate_weights: float32 [16384, 8], P(('expert', 'dp')), may hold values from 0.03 to 0.4
- latent_down: bfloat16 [4096, 1024], P('half', 'dp'), may hold values from -0.09375 to 0.09375
- latent_up: bfloat16 [1024, 4096], P('dp', 'half'), may hold values from -0.1875 to 0.1875
- expert_gate: bfloat16 [64, 1024, 1536], P('expert', 'dp', 'half'), may hold values from -0.1875 to 0.1875
- expert_linear: bfloat16 [64, 1024, 1536], P('expert', 'dp', 'half'), may hold values from -0.1875 to 0.1875
- expert_out: bfloat16 [64, 1536, 1024], P('expert', 'half', 'dp'), may hold values from -0.15625 to 0.15625
Outputs:
- token_grad: bfloat16 [16384, 4096], P(('expert', 'dp'), 'half')
- gate_grad: bfloat16 [64, 1024, 1536], P('expert', 'dp', 'half')
- linear_grad: bfloat16 [64, 1024, 1536], P('expert', 'dp', 'half')
- out_grad: bfloat16 [64, 1536, 1024], P('expert', 'half', 'dp')
Inputs may be any that keep to these rules, and one draw needn't show every extreme that they name: `expert_ids`: each row names 8 different experts. In each aligned block of 128 rows (the rows of one device) no expert is named by more than 18 rows, and one expert is named by exactly 18 rows in every block. `slot_ids`: within one aligned block of 128 rows, the entries that name the same expert have different slots.
All inputs are finite; a program needn't handle non-finite values.
Results may differ from a plain program's by a relative error of at most 0.013.
Values may be sent and summed in bfloat16 or wider, within the bound.
A program may use at most 128 MiB of HBM per device.

v0:
```python
import jax
import jax.numpy as jnp
from jax import lax
from jax.sharding import PartitionSpec as P


def on_device(
    tokens,
    cotangent,
    expert_ids,
    slot_ids,
    gate_weights,
    latent_down,
    latent_up,
    expert_gate,
    expert_linear,
    expert_out,
):
    row_count = tokens.shape[0]
    pick_count = expert_ids.shape[1]
    local_count = expert_gate.shape[0]
    group_count = lax.axis_size("expert")
    expert_count = group_count * local_count
    capacity = min(
        row_count, 2 * ((9 * row_count * pick_count + 16 * expert_count - 1) // (16 * expert_count))
    )
    down_full, up_full, gate_full, linear_full, output_full = (
        lax.all_gather(latent_down, "dp", axis=1, tiled=True),
        lax.all_gather(latent_up, "dp", axis=0, tiled=True),
        lax.all_gather(expert_gate, "dp", axis=1, tiled=True),
        lax.all_gather(expert_linear, "dp", axis=1, tiled=True),
        lax.all_gather(expert_out, "dp", axis=2, tiled=True),
    )
    latent_part = jnp.dot(tokens, down_full, preferred_element_type=jnp.float32)
    back_part = lax.dot_general(
        cotangent, up_full, (((1,), (1,)), ((), ())), preferred_element_type=jnp.float32
    )
    latent_sum, back_latent = lax.psum((latent_part, back_part), "half")
    latent = latent_sum.astype(jnp.bfloat16)
    width = latent.shape[1]
    flat_slot = (expert_ids * capacity + slot_ids).reshape(-1)
    slot_table = lax.broadcasted_iota(
        jnp.int32, (expert_count * capacity, row_count * pick_count), 0
    )
    matches = flat_slot[None, :] == slot_table
    choice_index = lax.broadcasted_iota(jnp.int32, matches.shape, 1)
    source = jnp.sum(jnp.where(matches, choice_index, 0), axis=1)
    filled = jnp.any(matches, axis=1)
    token_of = source // pick_count
    gate_of = gate_weights.reshape(-1)[source]
    send_latent = jnp.where(filled[:, None], latent[token_of], jnp.zeros((), jnp.bfloat16))
    send_back = jnp.where(filled[:, None], gate_of[:, None] * back_latent[token_of], 0.0).astype(
        jnp.bfloat16
    )
    send_latent = send_latent.reshape(group_count, local_count, capacity, width)
    send_back = send_back.reshape(group_count, local_count, capacity, width)
    rows_latent, rows_back = (
        lax.all_to_all(send_latent, "expert", split_axis=0, concat_axis=0, tiled=True),
        lax.all_to_all(send_back, "expert", split_axis=0, concat_axis=0, tiled=True),
    )
    pre_gate = jnp.einsum(
        "neci,eih->nech", rows_latent, gate_full, preferred_element_type=jnp.float32
    )
    pre_linear = jnp.einsum(
        "neci,eih->nech", rows_latent, linear_full, preferred_element_type=jnp.float32
    )
    grad_hidden = jnp.einsum(
        "necj,ehj->nech", rows_back, output_full, preferred_element_type=jnp.float32
    )
    logistic = jax.nn.sigmoid(pre_gate)
    hidden = (pre_gate * logistic * pre_linear).astype(jnp.bfloat16)
    gate_delta = (grad_hidden * pre_linear * logistic * (1.0 + pre_gate * (1.0 - logistic))).astype(
        jnp.bfloat16
    )
    linear_delta = (grad_hidden * pre_gate * logistic).astype(jnp.bfloat16)
    gate_part = jnp.einsum(
        "neci,nech->eih", rows_latent, gate_delta, preferred_element_type=jnp.float32
    )
    linear_part = jnp.einsum(
        "neci,nech->eih", rows_latent, linear_delta, preferred_element_type=jnp.float32
    )
    out_part = jnp.einsum("nech,necj->ehj", hidden, rows_back, preferred_element_type=jnp.float32)
    gate_share, linear_share, out_share = (
        lax.psum_scatter(
            gate_part.astype(jnp.bfloat16), "dp", scatter_dimension=1, tiled=True
        ).astype(jnp.float32),
        lax.psum_scatter(
            linear_part.astype(jnp.bfloat16), "dp", scatter_dimension=1, tiled=True
        ).astype(jnp.float32),
        lax.psum_scatter(
            out_part.astype(jnp.bfloat16), "dp", scatter_dimension=2, tiled=True
        ).astype(jnp.float32),
    )
    row_part = jnp.einsum(
        "nech,eih->neci", gate_delta, gate_full, preferred_element_type=jnp.float32
    )
    row_part = row_part + jnp.einsum(
        "nech,eih->neci", linear_delta, linear_full, preferred_element_type=jnp.float32
    )
    row_whole = lax.psum(row_part, "half").astype(jnp.bfloat16)
    returned = lax.all_to_all(row_whole, "expert", split_axis=0, concat_axis=0, tiled=True)
    position = expert_ids * capacity + slot_ids
    gathered = returned.reshape(expert_count * capacity, width)[position]
    latent_grad = jnp.sum(gathered.astype(jnp.float32), axis=1)
    token_grad = lax.dot_general(
        latent_grad.astype(jnp.bfloat16),
        down_full,
        (((1,), (1,)), ((), ())),
        preferred_element_type=jnp.float32,
    )
    return (
        token_grad.astype(jnp.bfloat16),
        gate_share.astype(jnp.bfloat16),
        linear_share.astype(jnp.bfloat16),
        out_share.astype(jnp.bfloat16),
    )


def solution(mesh):
    in_specs = (
        P(("expert", "dp"), "half"),
        P(("expert", "dp"), "half"),
        P(("expert", "dp"), None),
        P(("expert", "dp"), None),
        P(("expert", "dp"), None),
        P("half", "dp"),
        P("dp", "half"),
        P("expert", "dp", "half"),
        P("expert", "dp", "half"),
        P("expert", "half", "dp"),
    )
    out_specs = (
        P(("expert", "dp"), "half"),
        P("expert", "dp", "half"),
        P("expert", "dp", "half"),
        P("expert", "half", "dp"),
    )
    return jax.shard_map(
        on_device, mesh=mesh, in_specs=in_specs, out_specs=out_specs, check_vma=False
    )
```

profile of v0, /device:TPU:38, one launch (start us, length us, event | category | flops | bytes accessed | tf_op | source)
XLA Modules:
  0.0 497.7 jit_solution(3944161558312490674)
XLA Ops:
  7.2 0.0 all-gather.10.cloned.1.call-start
  7.2 0.7 all-gather.10.cloned.1.call-update
  7.9 0.0 all-gather.6.cloned.1.call-start
  8.0 0.7 all-gather.6.cloned.1.call-update
  8.7 0.1 copy.38
  8.8 0.1 eq.10
  8.9 0.6 fusion.2
  9.5 0.6 select_reduce_fusion
  10.1 0.1 broadcast_in_dim.37
  10.2 0.1 copy.39
  10.3 0.1 fusion.70
  10.4 21.0 %all-gather.10.cloned.1.call-done = bf16[2048,1024]{1,0:T(8,128)(2,1)} async-done(((bf16[2048,512]{1,0:T(8,128)(2,1)}), bf16[2048,1024]{1,0:T(8,128)(2,1)}) %all-gather.10.cloned.1.call-update) | async-done | bytes 4194320 | tf_op jit(solution)/shard_map/all_gather | solution.py:28
  31.4 2.9 fusion.74
  34.3 18.1 %all-reduce.5 = bf16[128,1024]{1,0:T(8,128)(2,1)S(1)} all-reduce(f32[128,1024]{1,0:T(8,128)S(1)} %fusion.74), channel_id=1, replica_groups=mesh['expert'=64,'half'=2,'dp'=2] {'half'}, use_global_device_ids=true, to_apply=%region_3.4 | all-reduce | flops 131072 | bytes 786432 | tf_op jit(solution)/shard_map/psum | solution.py:38
  52.4 4.4 gather_fusion.2
  56.8 2.4 gather.20
  59.3 4.7 copy_select_fusion
  63.9 3.1 copy.46
  67.0 12.9 %all-to-all-start.1 = ((bf16[64,1,18,1024]{3,2,1,0:T(8,128)(2,1)}), bf16[64,1,18,1024]{3,2,1,0:T(8,128)(2,1)}, u32[]{:S(2)}, u32[]{:S(2)}) async-start(bf16[64,1,18,1024]{3,2,1,0:T(8,128)(2,1)} %copy.46), calls=%async_computation.1 | async-start | bytes 6291456 | tf_op jit(solution)/shard_map/all_to_all | solution.py:58
  80.0 0.2 all-reduce.4.cloned.1.call-start
  80.2 0.0 all-gather.6.cloned.1.call-done
  80.2 4.5 fusion.73
  84.8 0.1 copy.40
  84.9 0.1 reshape.177
  85.0 4.6 gather_fusion
  89.5 0.1 mul.46
  89.7 0.1 copy.41
  89.7 50.7 %all-reduce.4.cloned.1.call-done = f32[128,1024]{1,0:T(8,128)} async-done(((f32[128,1024]{1,0:T(8,128)}), f32[128,1024]{1,0:T(8,128)}) %all-reduce.4.cloned.1.call-update) | async-done | bytes 524304 | tf_op jit(solution)/shard_map/psum | solution.py:38
  140.4 7.6 %gather_fusion.1 = f32[1152,1024]{1,0:T(8,128)} fusion(f32[128,1024]{1,0:T(8,128)} %all-reduce.4.cloned.1.call-done, s32[2048]{0:T(1024)S(1)} %pad_clamp_fusion), kind=kCustom, calls=%fused_computation.1 | custom fusion | bytes 9441792 | tf_op jit(solution)/shard_map/gather | solution.py:52
  148.1 5.6 %gather.18 = f32[64,1,18,1024]{3,2,0,1:T(8,128)} reshape(f32[1152,1024]{1,0:T(8,128)} %gather_fusion.1) | data formatting | bytes 9437184 | tf_op jit(solution)/shard_map/gather | solution.py:52
  153.6 5.6 %fusion.1 = bf16[64,1,18,1024]{3,0,2,1:T(8,128)(2,1)S(1)} fusion(f32[64,1,18,1024]{3,2,0,1:T(8,128)} %gather.18, f32[64,18]{0,1:T(8,128)S(1)} %copy.41, pred[64,18]{0,1:T(8,128)(4,1)S(1)} %copy.39), kind=kLoop, calls=%fused_computation.6 | loop fusion | flops 3538944 | bytes 7083648 | tf_op jit(solution)/shard_map/convert_element_type | solution.py:52
  159.3 3.0 copy.43
  162.3 10.3 %all-to-all-start = ((bf16[64,1,18,1024]{3,2,1,0:T(8,128)(2,1)}), bf16[64,1,18,1024]{3,2,1,0:T(8,128)(2,1)}, u32[]{:S(2)}, u32[]{:S(2)}) async-start(bf16[64,1,18,1024]{3,2,1,0:T(8,128)(2,1)} %copy.43), calls=%async_computation | async-start | bytes 6291456 | tf_op jit(solution)/shard_map/all_to_all | solution.py:59
  172.6 0.0 all-gather.14.cloned.1.call-start
  172.7 0.5 all-gather.14.cloned.1.call-update
  173.2 0.0 all-gather.12.cloned.1.call-start
  173.3 0.5 all-gather.12.cloned.1.call-update
  173.8 0.0 all-gather.8.cloned.1.call-start
  173.8 0.5 all-gather.8.cloned.1.call-update
  174.4 0.3 reduce-scatter.8.cloned.1.call-start
  174.6 16.8 %all-gather.14.cloned.1.call-done = bf16[1,1024,768]{2,1,0:T(8,128)(2,1)} async-done(((bf16[1,512,768]{2,1,0:T(8,128)(2,1)}), bf16[1,1024,768]{2,1,0:T(8,128)(2,1)}) %all-gather.14.cloned.1.call-update) | async-done | bytes 1572880 | tf_op jit(solution)/shard_map/all_gather | solution.py:30
  191.4 8.2 %fusion.17 = f32[64,18,768]{2,0,1:T(8,128)} fusion(bf16[1,1024,768]{2,1,0:T(8,128)(2,1)} %all-gather.14.cloned.1.call-done, bf16[64,1,18,1024]{3,2,1,0:T(8,128)(2,1)} %all-to-all-done.1), kind=kOutput, calls=%fused_computation.35 | convolution fusion | flops 1811939328 | bytes 7471104 | tf_op jit(solution)/shard_map/neci,eih->nech/dot_general | solution.py:61
  199.6 10.1 %all-gather.12.cloned.1.call-done = bf16[1,1024,768]{2,1,0:T(8,128)(2,1)} async-done(((bf16[1,512,768]{2,1,0:T(8,128)(2,1)}), bf16[1,1024,768]{2,1,0:T(8,128)(2,1)}) %all-gather.12.cloned.1.call-update) | async-done | bytes 1572880 | tf_op jit(solution)/shard_map/all_gather | solution.py:31
  209.7 8.2 %fusion.19 = f32[64,18,768]{2,0,1:T(8,128)} fusion(bf16[1,1024,768]{2,1,0:T(8,128)(2,1)} %all-gather.12.cloned.1.call-done, bf16[64,1,18,1024]{3,2,1,0:T(8,128)(2,1)} %all-to-all-done.1), kind=kOutput, calls=%fused_computation.37 | convolution fusion | flops 1811939328 | bytes 7471104 | tf_op jit(solution)/shard_map/neci,eih->nech/dot_general | solution.py:64
  217.9 30.1 %all-to-all-done = bf16[64,1,18,1024]{3,2,1,0:T(8,128)(2,1)} async-done(((bf16[64,1,18,1024]{3,2,1,0:T(8,128)(2,1)}), bf16[64,1,18,1024]{3,2,1,0:T(8,128)(2,1)}, u32[]{:S(2)}, u32[]{:S(2)}) %all-to-all-start) | async-done | bytes 2359328 | tf_op jit(solution)/shard_map/all_to_all | solution.py:59
  248.0 9.5 %fusion.61 = bf16[1,768,1024]{2,1,0:T(8,128)(2,1)} fusion(bf16[64,1,18,1024]{3,2,1,0:T(8,128)(2,1)} %all-to-all-done, f32[64,18,768]{2,0,1:T(8,128)} %fusion.19, f32[64,18,768]{2,0,1:T(8,128)} %fusion.17), kind=kOutput, calls=%fused_computation.60 | convolution fusion | flops 1818034176 | bytes 11010048 | tf_op jit(solution)/shard_map/nech,necj->ehj/dot_general | solution.py:82
  257.5 0.4 reduce-scatter.4.cloned.1.call-start
  258.0 0.0 all-gather.8.cloned.1.call-done
  258.0 9.3 %fusion.8 = (bf16[64,1,18,768]{3,0,2,1:T(8,128)(2,1)S(1)}, bf16[64,1,18,768]{3,0,2,1:T(8,128)(2,1)S(1)}) fusion(f32[64,18,768]{2,0,1:T(8,128)} %fusion.17, f32[64,18,768]{2,0,1:T(8,128)} %fusion.19, bf16[1,768,1024]{2,1,0:T(8,128)(2,1)} %all-gather.8.cloned.1.call-done, bf16[64,1,18,1024]{3,2,1,0:T(8,128)(2,1)} %all-to-all-done), kind=kOutput, calls=%fused_computation.19 | convolution fusion | flops 1823440896 | bytes 14548992 | tf_op jit(solution)/shard_map/necj,ehj->nech/dot_general | solution.py:67
  267.3 2.1 fusion.29
  269.4 4.2 add_bitcast_fusion
  273.6 6.1 %fusion.51 = bf16[1,1024,768]{2,1,0:T(8,128)(2,1)} fusion(bf16[64,1,18,768]{3,0,2,1:T(8,128)(2,1)S(1)} %get-tuple-element.9, bf16[64,1,18,1024]{3,2,1,0:T(8,128)(2,1)} %all-to-all-done.1), kind=kOutput, calls=%fused_computation.58 | convolution fusion | flops 1812725760 | bytes 5701632 | tf_op jit(solution)/shard_map/neci,nech->eih/dot_general | solution.py:76
  279.8 109.2 %all-reduce.6 = bf16[64,1,18,1024]{3,0,2,1:T(8,128)(2,1)S(1)} all-reduce(f32[64,1,18,1024]{3,0,2,1:T(8,128)} %add_bitcast_fusion), channel_id=1, replica_groups=mesh['expert'=64,'half'=2,'dp'=2] {'half'}, use_global_device_ids=true, to_apply=%region_4.5 | all-reduce | flops 1179648 | bytes 7077888 | tf_op jit(solution)/shard_map/psum | solution.py:100
  389.0 3.0 copy.48
  392.0 9.3 %all-to-all-start.2 = ((bf16[64,1,18,1024]{3,2,1,0:T(8,128)(2,1)}), bf16[64,1,18,1024]{3,2,1,0:T(8,128)(2,1)}, u32[]{:S(2)}, u32[]{:S(2)}) async-start(bf16[64,1,18,1024]{3,2,1,0:T(8,128)(2,1)} %copy.48), calls=%async_computation.2 | async-start | bytes 6291456 | tf_op jit(solution)/shard_map/all_to_all | solution.py:101
  401.3 0.0 reduce-scatter.6.cloned.1.call-start
  401.4 6.0 %fusion.56 = bf16[1,1024,768]{2,1,0:T(8,128)(2,1)} fusion(bf16[64,1,18,768]{3,0,2,1:T(8,128)(2,1)S(1)} %copy-done.9, bf16[64,1,18,1024]{3,2,1,0:T(8,128)(2,1)} %all-to-all-done.1), kind=kOutput, calls=%fused_computation.59 | convolution fusion | flops 1812725760 | bytes 5701632 | tf_op jit(solution)/shard_map/neci,nech->eih/dot_general | solution.py:79
  407.4 0.1 copy.49
  407.5 0.1 reshape.213
  407.6 67.5 %all-to-all-done.2 = bf16[64,1,18,1024]{3,2,1,0:T(8,128)(2,1)} async-done(((bf16[64,1,18,1024]{3,2,1,0:T(8,128)(2,1)}), bf16[64,1,18,1024]{3,2,1,0:T(8,128)(2,1)}, u32[]{:S(2)}, u32[]{:S(2)}) %all-to-all-start.2) | async-done | bytes 2359328 | tf_op jit(solution)/shard_map/all_to_all | solution.py:101
  475.1 2.9 reshape.185
  478.1 5.4 %gather_fusion.3 = bf16[1024,1024]{1,0:T(8,128)(2,1)} fusion(bf16[1152,1024]{1,0:T(8,128)(2,1)S(1)} %reshape.185, s32[1024]{0:T(1024)S(1)} %broadcast_clamp_fusion), kind=kCustom, calls=%fused_computation.3 | custom fusion | bytes 4198400 | tf_op jit(solution)/shard_map/gather | solution.py:103
  483.4 3.0 bitcast_reduce_fusion
  486.5 4.5 convolution_convert_fusion
  (32 shorter events, 0.2 us)
Async XLA Ops:
  7.2 24.3 %copy-start = (bf16[128,2048]{1,0:T(8,128)(2,1)S(1)}, bf16[128,2048]{1,0:T(8,128)(2,1)}, u32[]{:S(2)}) copy-start(bf16[128,2048]{1,0:T(8,128)(2,1)} %param.10) | copy-start | bytes 1572868
  7.2 1.5 copy-start.4
  7.2 1.5 copy-start.5
  7.2 24.2 %all-gather.10.cloned.1.call-start = ((), (), s32[]{:S(2)}) async-start(), calls=%async_computation.9 | async-start | bytes 6291456 | tf_op jit(solution)/shard_map/all_gather | solution.py:28
  7.9 72.3 %all-gather.6.cloned.1.call-start = ((), (), s32[]{:S(2)}) async-start(), calls=%async_computation.6 | async-start | bytes 6291456 | tf_op jit(solution)/shard_map/all_gather | solution.py:29
  67.0 13.2 %copy-start.2 = (bf16[128,2048]{1,0:T(8,128)(2,1)S(1)}, bf16[128,2048]{1,0:T(8,128)(2,1)}, u32[]{:S(2)}) copy-start(bf16[128,2048]{1,0:T(8,128)(2,1)} %param.11) | copy-start | bytes 1572868
  67.0 95.3 %all-to-all-start.1 = ((bf16[64,1,18,1024]{3,2,1,0:T(8,128)(2,1)}), bf16[64,1,18,1024]{3,2,1,0:T(8,128)(2,1)}, u32[]{:S(2)}, u32[]{:S(2)}) async-start(bf16[64,1,18,1024]{3,2,1,0:T(8,128)(2,1)} %copy.46), calls=%async_computation.1 | async-start | bytes 6291456 | tf_op jit(solution)/shard_map/all_to_all | solution.py:58
  79.9 4.8 copy-start.3
  80.0 60.5 %all-reduce.4.cloned.1.call-start = ((), (), s32[]{:S(2)}) async-start(), calls=%async_computation.7 | async-start | bytes 1048576 | tf_op jit(solution)/shard_map/psum | solution.py:38
  162.3 85.7 %all-to-all-start = ((bf16[64,1,18,1024]{3,2,1,0:T(8,128)(2,1)}), bf16[64,1,18,1024]{3,2,1,0:T(8,128)(2,1)}, u32[]{:S(2)}, u32[]{:S(2)}) async-start(bf16[64,1,18,1024]{3,2,1,0:T(8,128)(2,1)} %copy.43), calls=%async_computation | async-start | bytes 6291456 | tf_op jit(solution)/shard_map/all_to_all | solution.py:59
  172.6 18.8 %all-gather.14.cloned.1.call-start = ((), (), s32[]{:S(2)}) async-start(), calls=%async_computation.11 | async-start | bytes 2359296 | tf_op jit(solution)/shard_map/all_gather | solution.py:30
  173.2 36.5 %all-gather.12.cloned.1.call-start = ((), (), s32[]{:S(2)}) async-start(), calls=%async_computation.10 | async-start | bytes 2359296 | tf_op jit(solution)/shard_map/all_gather | solution.py:31
  173.8 84.2 %all-gather.8.cloned.1.call-start = ((), (), s32[]{:S(2)}) async-start(), calls=%async_computation.8 | async-start | bytes 2359296 | tf_op jit(solution)/shard_map/all_gather | solution.py:32
  174.4 316.6 %reduce-scatter.8.cloned.1.call-start = ((), (), s32[]{:S(2)}) async-start(), calls=%async_computation.14 | async-start | bytes 2359296 | tf_op jit(solution)/shard_map/reduce_scatter | solution.py:90
  257.5 9.8 %copy-start.6 = (bf16[1,1024,768]{2,1,0:T(8,128)(2,1)S(1)}, bf16[1,1024,768]{2,1,0:T(8,128)(2,1)}, u32[]{:S(2)}) copy-start(bf16[1,1024,768]{2,1,0:T(8,128)(2,1)} %all-gather.14.cloned.1.call-done) | copy-start | bytes 4718596
  257.5 233.5 %reduce-scatter.4.cloned.1.call-start = ((), (), s32[]{:S(2)}) async-start(), calls=%async_computation.12 | async-start | bytes 2359296 | tf_op jit(solution)/shard_map/reduce_scatter | solution.py:84
  267.3 2.1 copy-start.8
  267.3 2.1 copy-start.7
  392.0 9.4 %copy-start.9 = (bf16[64,1,18,768]{3,0,2,1:T(8,128)(2,1)S(1)}, bf16[64,1,18,768]{3,0,2,1:T(8,128)(2,1)}, u32[]{:S(2)}) copy-start(bf16[64,1,18,768]{3,0,2,1:T(8,128)(2,1)} %copy-done.8) | copy-start | bytes 5308420
  392.0 83.1 %all-to-all-start.2 = ((bf16[64,1,18,1024]{3,2,1,0:T(8,128)(2,1)}), bf16[64,1,18,1024]{3,2,1,0:T(8,128)(2,1)}, u32[]{:S(2)}, u32[]{:S(2)}) async-start(bf16[64,1,18,1024]{3,2,1,0:T(8,128)(2,1)} %copy.48), calls=%async_computation.2 | async-start | bytes 6291456 | tf_op jit(solution)/shard_map/all_to_all | solution.py:101
  401.3 89.7 %reduce-scatter.6.cloned.1.call-start = ((), (), s32[]{:S(2)}) async-start(), calls=%async_computation.13 | async-start | bytes 2359296 | tf_op jit(solution)/shard_map/reduce_scatter | solution.py:87
  478.1 12.9 %copy-start.1 = (bf16[128,2048]{1,0:T(8,128)(2,1)S(1)}, bf16[128,2048]{1,0:T(8,128)(2,1)}, u32[]{:S(2)}) copy-start(bf16[128,2048]{1,0:T(8,128)(2,1)} %param.10) | copy-start | bytes 1572868
Sparse Core Ops, SparseCore 0:
  9.8 21.5 all-gather.9
  33.2 20.2 all-gather.5
  84.9 55.5 all-reduce.3
  175.1 16.2 all-gather.13
  193.2 16.4 all-gather.11
  211.5 16.4 all-gather.7
  257.6 8.8 reduce-scatter.7
  279.9 8.8 reduce-scatter.3
  407.6 15.5 reduce-scatter.5
where the time goes:
time: 505 us; the launch traced here: 498 us
  waiting for transfers between devices  199 us (39%)
  blocking collectives  127 us (25%)
  matrix products  65.5 us (13%)
  local copies, waits for them, and re-layouts  43.1 us (9%)
  starting transfers between devices  33.7 us (7%)
  other arithmetic  14.6 us (3%)
  between operations  14.3 us (3%)
    psum x1, blocking collectives, on_device(): row_whole = lax.psum(row_part, 'half').astype(jnp.bfloat16)  109 us
    all_to_all x1, waiting for transfers between devices, on_device(): lax.all_to_all(row_whole, 'expert', split_axis=0, concat_axis=0, tiled=True)  67.5 us
    psum x1, waiting for transfers between devices, on_device(): latent_sum, back_latent = lax.psum((latent_part, back_part), 'half')  50.7 us
    all_to_all x1, waiting for transfers between devices, on_device(): lax.all_to_all(send_back, 'expert', split_axis=0, concat_axis=0, tiled=True)  30.1 us
    all_gather x1, waiting for transfers between devices, on_device(): lax.all_gather(latent_down, 'dp', axis=1, tiled=True)  21 us
    psum x1, blocking collectives, on_device(): latent_sum, back_latent = lax.psum((latent_part, back_part), 'half')  18.1 us
    all_gather x1, waiting for transfers between devices, on_device(): lax.all_gather(expert_gate, 'dp', axis=1, tiled=True)  16.8 us
    gather x2, local copies, waits for them, and re-layouts, on_device(): back_latent[token_of]  13.2 us
  transfers between devices with their start and end apart: 12, of which 6 were waited for; matrix products, arithmetic and copies ran while one was open for 25% of the time, Pallas kernels for 0%

commit v1 on v0

--- a/solution.py
+++ b/solution.py
@@ -2,6 +2,11 @@
 import jax.numpy as jnp
 from jax import lax
 from jax.sharding import PartitionSpec as P
+
+
+def tiled_gather(value, axis, dim):
+    copies = jnp.concatenate([value] * lax.axis_size(axis), axis=dim)
+    return lax.all_to_all(copies, axis, dim, dim, tiled=True)
 
 
 def on_device(
@@ -25,7 +30,7 @@
         row_count, 2 * ((9 * row_count * pick_count + 16 * expert_count - 1) // (16 * expert_count))
     )
     down_full, up_full, gate_full, linear_full, output_full = (
-        lax.all_gather(latent_down, "dp", axis=1, tiled=True),
+        tiled_gather(latent_down, "dp", 1),
         lax.all_gather(latent_up, "dp", axis=0, tiled=True),
         lax.all_gather(expert_gate, "dp", axis=1, tiled=True),
         lax.all_gather(expert_linear, "dp", axis=1, tiled=True),

time: 505 us -> 517 us (1.024)
  waiting for transfers between devices: 199 us -> 182 us
  local copies, waits for them, and re-layouts: 43.1 us -> 58.8 us
  starting transfers between devices: 33.7 us -> 43.5 us
    all_gather x1 -> x0, waiting for transfers between devices: 21 us -> none  [on_device(): lax.all_gather(latent_down, 'dp', axis=1, tiled=True)]
    all_to_all x0 -> x2, local copies, waits for them, and re-layouts: none -> 12.5 us  [tiled_gather(): return lax.all_to_all(copies, axis, dim, dim, tiled=True)]
    all_to_all x0 -> x1, starting transfers between devices: none -> 5.84 us  [tiled_gather(): return lax.all_to_all(copies, axis, dim, dim, tiled=True)]
  transfers between devices with their start and end apart: 12 -> 12, of which waited for: 6 -> 6; matrix products, arithmetic and copies ran while one was open for 25% -> 28% of each run, Pallas kernels for 0% -> 0%
where the time goes in v1:
time: 517 us; the launch traced here: 508 us
  waiting for transfers between devices  182 us (35%)
  blocking collectives  127 us (25%)
  matrix products  65.2 us (13%)
  local copies, waits for them, and re-layouts  58.8 us (11%)
  starting transfers between devices  43.5 us (8%)
  other arithmetic  17.1 us (3%)
  between operations  14.6 us (3%)
    psum x1, blocking collectives, on_device(): row_whole = lax.psum(row_part, 'half').astype(jnp.bfloat16)  109 us
    all_to_all x1, waiting for transfers between devices, on_device(): lax.all_to_all(row_whole, 'expert', split_axis=0, concat_axis=0, tiled=True)  67.5 us
    psum x1, waiting for transfers between devices, on_device(): latent_sum, back_latent = lax.psum((latent_part, back_part), 'half')  50.6 us
    all_to_all x1, waiting for transfers between devices, on_device(): lax.all_to_all(send_back, 'expert', split_axis=0, concat_axis=0, tiled=True)  29.8 us
    psum x1, blocking collectives, on_device(): latent_sum, back_latent = lax.psum((latent_part, back_part), 'half')  17.8 us
    all_gather x1, waiting for transfers between devices, on_device(): lax.all_gather(expert_gate, 'dp', axis=1, tiled=True)  16.9 us
    all_to_all x1, starting transfers between devices, on_device(): lax.all_to_all(send_latent, 'expert', split_axis=0, concat_axis=0, tiled=...  16.6 us
    gather x2, local copies, waits for them, and re-layouts, on_device(): back_latent[token_of]  13.3 us
  transfers between devices with their start and end apart: 12, of which 6 were waited for; matrix products, arithmetic and copies ran while one was open for 28% of the time, Pallas kernels for 0%

profile of v1, /device:TPU:38, one launch (start us, length us, event | category | flops | bytes accessed | tf_op | source)
XLA Modules:
  0.0 508.0 jit_solution(6533873796283148021)
XLA Ops:
  7.2 0.7 all-gather.5.cloned.1.call-update
  7.9 2.9 copy.66
  10.9 2.6 pad_maximum_fusion
  13.4 6.2 %copy.68 = bf16[2048,2,512]{2,0,1:T(8,128)(2,1)} copy(bf16[2048,2,512]{0,2,1:T(8,128)(2,1)} %bitcast.176) | data formatting | bytes 8388608 | tf_op jit(solution)/shard_map/all_to_all | solution.py:9
  19.6 5.8 %all-to-all-start.1 = ((bf16[2048,2,512]{2,0,1:T(8,128)(2,1)}), bf16[2048,2,512]{2,0,1:T(8,128)(2,1)}, u32[]{:S(2)}, u32[]{:S(2)}) async-start(bf16[2048,2,512]{2,0,1:T(8,128)(2,1)} %copy.68), calls=%async_computation.1 | async-start | bytes 8388608 | tf_op jit(solution)/shard_map/all_to_all | solution.py:9
  25.5 0.1 copy.59
  25.6 0.1 eq.10
  25.7 4.3 all-to-all-done.1
  30.0 6.3 %copy.69 = bf16[2048,2,512]{0,2,1:T(8,128)(2,1)} copy(bf16[2048,2,512]{2,0,1:T(8,128)(2,1)} %all-to-all-done.1) | data formatting | bytes 8388608 | tf_op jit(solution)/shard_map/all_to_all | solution.py:9
  36.2 3.4 convolution_bitcast_fusion
  39.7 17.8 %all-reduce.5 = bf16[128,1024]{0,1:T(8,128)(2,1)S(1)} all-reduce(f32[128,1024]{0,1:T(8,128)S(1)} %convolution_bitcast_fusion), channel_id=1, replica_groups=mesh['expert'=64,'half'=2,'dp'=2] {'half'}, use_global_device_ids=true, to_apply=%region_3.4 | all-reduce | flops 131072 | bytes 786432 | tf_op jit(solution)/shard_map/psum | solution.py:43
  57.5 0.6 fusion.2
  58.2 0.2 broadcast_in_dim.37
  58.3 0.1 copy.60
  58.4 0.2 copy.70
  58.6 0.6 select_reduce_fusion
  59.1 0.1 fusion.70
  59.2 4.4 gather_fusion.2
  63.6 2.4 gather.20
  66.0 4.7 copy_select_fusion
  70.7 3.1 copy.72
  73.8 16.6 %all-to-all-start.2 = ((bf16[64,1,18,1024]{3,2,1,0:T(8,128)(2,1)}), bf16[64,1,18,1024]{3,2,1,0:T(8,128)(2,1)}, u32[]{:S(2)}, u32[]{:S(2)}) async-start(bf16[64,1,18,1024]{3,2,1,0:T(8,128)(2,1)} %copy.72), calls=%async_computation.2 | async-start | bytes 6291456 | tf_op jit(solution)/shard_map/all_to_all | solution.py:63
  90.4 0.2 all-reduce.4.cloned.1.call-start
  90.7 4.5 fusion.73
  95.2 0.1 copy.61
  95.3 0.1 reshape.179
  95.4 4.6 gather_fusion
  100.0 0.1 mul.46
  100.1 0.1 copy.62
  100.2 50.6 %all-reduce.4.cloned.1.call-done = f32[128,1024]{1,0:T(8,128)} async-done(((f32[128,1024]{1,0:T(8,128)}), f32[128,1024]{1,0:T(8,128)}) %all-reduce.4.cloned.1.call-update) | async-done | bytes 524304 | tf_op jit(solution)/shard_map/psum | solution.py:43
  150.8 7.6 %gather_fusion.1 = f32[1152,1024]{1,0:T(8,128)} fusion(f32[128,1024]{1,0:T(8,128)} %all-reduce.4.cloned.1.call-done, s32[2048]{0:T(1024)S(1)} %pad_clamp_fusion), kind=kCustom, calls=%fused_computation.1 | custom fusion | bytes 9441792 | tf_op jit(solution)/shard_map/gather | solution.py:57
  158.5 5.6 %gather.18 = f32[64,1,18,1024]{3,2,0,1:T(8,128)} reshape(f32[1152,1024]{1,0:T(8,128)} %gather_fusion.1) | data formatting | bytes 9437184 | tf_op jit(solution)/shard_map/gather | solution.py:57
  164.1 5.6 %fusion.1 = bf16[64,1,18,1024]{3,0,2,1:T(8,128)(2,1)S(1)} fusion(f32[64,1,18,1024]{3,2,0,1:T(8,128)} %gather.18, f32[64,18]{0,1:T(8,128)S(1)} %copy.62, pred[64,18]{0,1:T(8,128)(4,1)S(1)} %copy.60), kind=kLoop, calls=%fused_computation.6 | loop fusion | flops 3538944 | bytes 7083648 | tf_op jit(solution)/shard_map/convert_element_type | solution.py:57
  169.8 3.0 copy.64
  172.8 10.3 %all-to-all-start = ((bf16[64,1,18,1024]{3,2,1,0:T(8,128)(2,1)}), bf16[64,1,18,1024]{3,2,1,0:T(8,128)(2,1)}, u32[]{:S(2)}, u32[]{:S(2)}) async-start(bf16[64,1,18,1024]{3,2,1,0:T(8,128)(2,1)} %copy.64), calls=%async_computation | async-start | bytes 6291456 | tf_op jit(solution)/shard_map/all_to_all | solution.py:64
  183.2 0.0 all-gather.11.cloned.1.call-start
  183.2 0.7 all-gather.11.cloned.1.call-update
  183.9 0.5 all-gather.9.cloned.1.call-update
  184.5 0.0 all-gather.7.cloned.1.call-start
  184.5 0.5 all-gather.7.cloned.1.call-update
  185.1 0.3 reduce-scatter.8.cloned.1.call-start
  185.3 16.9 %all-gather.11.cloned.1.call-done = bf16[1,1024,768]{2,1,0:T(8,128)(2,1)} async-done(((bf16[1,512,768]{2,1,0:T(8,128)(2,1)}), bf16[1,1024,768]{2,1,0:T(8,128)(2,1)}) %all-gather.11.cloned.1.call-update) | async-done | bytes 1572880 | tf_op jit(solution)/shard_map/all_gather | solution.py:35
  202.3 8.2 %fusion.17 = f32[64,18,768]{2,0,1:T(8,128)} fusion(bf16[1,1024,768]{2,1,0:T(8,128)(2,1)} %all-gather.11.cloned.1.call-done, bf16[64,1,18,1024]{3,2,1,0:T(8,128)(2,1)} %all-to-all-done.2), kind=kOutput, calls=%fused_computation.36 | convolution fusion | flops 1811939328 | bytes 7471104 | tf_op jit(solution)/shard_map/neci,eih->nech/dot_general | solution.py:66
  210.4 10.1 %all-gather.9.cloned.1.call-done = bf16[1,1024,768]{2,1,0:T(8,128)(2,1)} async-done(((bf16[1,512,768]{2,1,0:T(8,128)(2,1)}), bf16[1,1024,768]{2,1,0:T(8,128)(2,1)}) %all-gather.9.cloned.1.call-update) | async-done | bytes 1572880 | tf_op jit(solution)/shard_map/all_gather | solution.py:36
  220.5 8.2 %fusion.19 = f32[64,18,768]{2,0,1:T(8,128)} fusion(bf16[1,1024,768]{2,1,0:T(8,128)(2,1)} %all-gather.9.cloned.1.call-done, bf16[64,1,18,1024]{3,2,1,0:T(8,128)(2,1)} %all-to-all-done.2), kind=kOutput, calls=%fused_computation.38 | convolution fusion | flops 1811939328 | bytes 7471104 | tf_op jit(solution)/shard_map/neci,eih->nech/dot_general | solution.py:69
  228.7 29.8 %all-to-all-done = bf16[64,1,18,1024]{3,2,1,0:T(8,128)(2,1)} async-done(((bf16[64,1,18,1024]{3,2,1,0:T(8,128)(2,1)}), bf16[64,1,18,1024]{3,2,1,0:T(8,128)(2,1)}, u32[]{:S(2)}, u32[]{:S(2)}) %all-to-all-start) | async-done | bytes 2359328 | tf_op jit(solution)/shard_map/all_to_all | solution.py:64
  258.5 9.5 %fusion.61 = bf16[1,768,1024]{2,1,0:T(8,128)(2,1)} fusion(bf16[64,1,18,1024]{3,2,1,0:T(8,128)(2,1)} %all-to-all-done, f32[64,18,768]{2,0,1:T(8,128)} %fusion.19, f32[64,18,768]{2,0,1:T(8,128)} %fusion.17), kind=kOutput, calls=%fused_computation.61 | convolution fusion | flops 1818034176 | bytes 11010048 | tf_op jit(solution)/shard_map/nech,necj->ehj/dot_general | solution.py:87
  268.0 0.4 reduce-scatter.4.cloned.1.call-start
  268.5 9.3 %fusion.8 = (bf16[64,1,18,768]{3,0,2,1:T(8,128)(2,1)S(1)}, bf16[64,1,18,768]{3,0,2,1:T(8,128)(2,1)S(1)}) fusion(f32[64,18,768]{2,0,1:T(8,128)} %fusion.17, f32[64,18,768]{2,0,1:T(8,128)} %fusion.19, bf16[1,768,1024]{2,1,0:T(8,128)(2,1)} %all-gather.7.cloned.1.call-done, bf16[64,1,18,1024]{3,2,1,0:T(8,128)(2,1)} %all-to-all-done), kind=kOutput, calls=%fused_computation.20 | convolution fusion | flops 1823440896 | bytes 14548992 | tf_op jit(solution)/shard_map/necj,ehj->nech/dot_general | solution.py:72
  277.9 2.1 fusion.29
  280.0 4.2 add_bitcast_fusion
  284.2 6.1 %fusion.51 = bf16[1,1024,768]{2,1,0:T(8,128)(2,1)} fusion(bf16[64,1,18,768]{3,0,2,1:T(8,128)(2,1)S(1)} %get-tuple-element.9, bf16[64,1,18,1024]{3,2,1,0:T(8,128)(2,1)} %all-to-all-done.2), kind=kOutput, calls=%fused_computation.59 | convolution fusion | flops 1812725760 | bytes 5701632 | tf_op jit(solution)/shard_map/neci,nech->eih/dot_general | solution.py:81
  290.3 109.2 %all-reduce.6 = bf16[64,1,18,1024]{3,0,2,1:T(8,128)(2,1)S(1)} all-reduce(f32[64,1,18,1024]{3,0,2,1:T(8,128)} %add_bitcast_fusion), channel_id=1, replica_groups=mesh['expert'=64,'half'=2,'dp'=2] {'half'}, use_global_device_ids=true, to_apply=%region_4.5 | all-reduce | flops 1179648 | bytes 7077888 | tf_op jit(solution)/shard_map/psum | solution.py:105
  399.5 3.0 copy.74
  402.5 9.6 %all-to-all-start.3 = ((bf16[64,1,18,1024]{3,2,1,0:T(8,128)(2,1)}), bf16[64,1,18,1024]{3,2,1,0:T(8,128)(2,1)}, u32[]{:S(2)}, u32[]{:S(2)}) async-start(bf16[64,1,18,1024]{3,2,1,0:T(8,128)(2,1)} %copy.74), calls=%async_computation.3 | async-start | bytes 6291456 | tf_op jit(solution)/shard_map/all_to_all | solution.py:106
  412.1 0.0 reduce-scatter.6.cloned.1.call-start
  412.2 6.0 %fusion.56 = bf16[1,1024,768]{2,1,0:T(8,128)(2,1)} fusion(bf16[64,1,18,768]{3,0,2,1:T(8,128)(2,1)S(1)} %copy-done.9, bf16[64,1,18,1024]{3,2,1,0:T(8,128)(2,1)} %all-to-all-done.2), kind=kOutput, calls=%fused_computation.60 | convolution fusion | flops 1812725760 | bytes 5701632 | tf_op jit(solution)/shard_map/neci,nech->eih/dot_general | solution.py:84
  418.2 0.1 copy.75
  418.3 0.1 reshape.215
  418.4 67.5 %all-to-all-done.3 = bf16[64,1,18,1024]{3,2,1,0:T(8,128)(2,1)} async-done(((bf16[64,1,18,1024]{3,2,1,0:T(8,128)(2,1)}), bf16[64,1,18,1024]{3,2,1,0:T(8,128)(2,1)}, u32[]{:S(2)}, u32[]{:S(2)}) %all-to-all-start.3) | async-done | bytes 2359328 | tf_op jit(solution)/shard_map/all_to_all | solution.py:106
  485.9 2.9 reshape.187
  488.8 5.4 %gather_fusion.3 = bf16[1024,1024]{1,0:T(8,128)(2,1)} fusion(bf16[1152,1024]{1,0:T(8,128)(2,1)S(1)} %reshape.187, s32[1024]{0:T(1024)S(1)} %broadcast_clamp_fusion), kind=kCustom, calls=%fused_computation.3 | custom fusion | bytes 4198400 | tf_op jit(solution)/shard_map/gather | solution.py:108
  494.2 3.0 bitcast_reduce_fusion
  497.2 3.7 convolution_convert_fusion
  (36 shorter events, 0.3 us)
Async XLA Ops:
  7.2 29.1 %copy-start = (bf16[128,2048]{1,0:T(8,128)(2,1)S(1)}, bf16[128,2048]{1,0:T(8,128)(2,1)}, u32[]{:S(2)}) copy-start(bf16[128,2048]{1,0:T(8,128)(2,1)} %param.10) | copy-start | bytes 1572868
  7.2 83.5 %all-gather.5.cloned.1.call-start = ((), (), s32[]{:S(2)}) async-start(), calls=%async_computation.7 | async-start | bytes 6291456 | tf_op jit(solution)/shard_map/all_gather | solution.py:34
  19.6 5.9 %copy-start.4 = (s32[128,8]{0,1:T(8,128)S(1)}, s32[128,8]{0,1:T(8,128)}, u32[]{:S(2)}) copy-start(s32[128,8]{0,1:T(8,128)} %param.13) | copy-start | bytes 12292
  19.6 5.9 %copy-start.5 = (s32[128,8]{0,1:T(8,128)S(1)}, s32[128,8]{0,1:T(8,128)}, u32[]{:S(2)}) copy-start(s32[128,8]{0,1:T(8,128)} %param.12) | copy-start | bytes 12292
  19.6 10.3 %all-to-all-start.1 = ((bf16[2048,2,512]{2,0,1:T(8,128)(2,1)}), bf16[2048,2,512]{2,0,1:T(8,128)(2,1)}, u32[]{:S(2)}, u32[]{:S(2)}) async-start(bf16[2048,2,512]{2,0,1:T(8,128)(2,1)} %copy.68), calls=%async_computation.1 | async-start | bytes 8388608 | tf_op jit(solution)/shard_map/all_to_all | solution.py:9
  73.8 16.9 %copy-start.2 = (bf16[128,2048]{1,0:T(8,128)(2,1)S(1)}, bf16[128,2048]{1,0:T(8,128)(2,1)}, u32[]{:S(2)}) copy-start(bf16[128,2048]{1,0:T(8,128)(2,1)} %param.11) | copy-start | bytes 1572868
  73.8 99.0 %all-to-all-start.2 = ((bf16[64,1,18,1024]{3,2,1,0:T(8,128)(2,1)}), bf16[64,1,18,1024]{3,2,1,0:T(8,128)(2,1)}, u32[]{:S(2)}, u32[]{:S(2)}) async-start(bf16[64,1,18,1024]{3,2,1,0:T(8,128)(2,1)} %copy.72), calls=%async_computation.2 | async-start | bytes 6291456 | tf_op jit(solution)/shard_map/all_to_all | solution.py:63
  90.4 4.8 copy-start.3
  90.4 60.4 %all-reduce.4.cloned.1.call-start = ((), (), s32[]{:S(2)}) async-start(), calls=%async_computation.8 | async-start | bytes 1048576 | tf_op jit(solution)/shard_map/psum | solution.py:43
  172.8 85.7 %all-to-all-start = ((bf16[64,1,18,1024]{3,2,1,0:T(8,128)(2,1)}), bf16[64,1,18,1024]{3,2,1,0:T(8,128)(2,1)}, u32[]{:S(2)}, u32[]{:S(2)}) async-start(bf16[64,1,18,1024]{3,2,1,0:T(8,128)(2,1)} %copy.64), calls=%async_computation | async-start | bytes 6291456 | tf_op jit(solution)/shard_map/all_to_all | solution.py:64
  183.2 19.1 %all-gather.11.cloned.1.call-start = ((), (), s32[]{:S(2)}) async-start(), calls=%async_computation.11 | async-start | bytes 2359296 | tf_op jit(solution)/shard_map/all_gather | solution.py:35
  183.9 36.6 %all-gather.9.cloned.1.call-start = ((), (), s32[]{:S(2)}) async-start(), calls=%async_computation.10 | async-start | bytes 2359296 | tf_op jit(solution)/shard_map/all_gather | solution.py:36
  184.5 84.0 %all-gather.7.cloned.1.call-start = ((), (), s32[]{:S(2)}) async-start(), calls=%async_computation.9 | async-start | bytes 2359296 | tf_op jit(solution)/shard_map/all_gather | solution.py:37
  185.1 315.9 %reduce-scatter.8.cloned.1.call-start = ((), (), s32[]{:S(2)}) async-start(), calls=%async_computation.14 | async-start | bytes 2359296 | tf_op jit(solution)/shard_map/reduce_scatter | solution.py:95
  268.0 9.8 %copy-start.6 = (bf16[1,1024,768]{2,1,0:T(8,128)(2,1)S(1)}, bf16[1,1024,768]{2,1,0:T(8,128)(2,1)}, u32[]{:S(2)}) copy-start(bf16[1,1024,768]{2,1,0:T(8,128)(2,1)} %all-gather.11.cloned.1.call-done) | copy-start | bytes 4718596
  268.0 232.9 %reduce-scatter.4.cloned.1.call-start = ((), (), s32[]{:S(2)}) async-start(), calls=%async_computation.12 | async-start | bytes 2359296 | tf_op jit(solution)/shard_map/reduce_scatter | solution.py:89
  277.9 2.1 copy-start.8
  277.9 2.1 copy-start.7
  402.5 9.6 %copy-start.9 = (bf16[64,1,18,768]{3,0,2,1:T(8,128)(2,1)S(1)}, bf16[64,1,18,768]{3,0,2,1:T(8,128)(2,1)}, u32[]{:S(2)}) copy-start(bf16[64,1,18,768]{3,0,2,1:T(8,128)(2,1)} %copy-done.8) | copy-start | bytes 5308420
  402.5 83.4 %all-to-all-start.3 = ((bf16[64,1,18,1024]{3,2,1,0:T(8,128)(2,1)}), bf16[64,1,18,1024]{3,2,1,0:T(8,128)(2,1)}, u32[]{:S(2)}, u32[]{:S(2)}) async-start(bf16[64,1,18,1024]{3,2,1,0:T(8,128)(2,1)} %copy.74), calls=%async_computation.3 | async-start | bytes 6291456 | tf_op jit(solution)/shard_map/all_to_all | solution.py:106
  412.1 88.9 %reduce-scatter.6.cloned.1.call-start = ((), (), s32[]{:S(2)}) async-start(), calls=%async_computation.13 | async-start | bytes 2359296 | tf_op jit(solution)/shard_map/reduce_scatter | solution.py:92
  488.8 12.1 %copy-start.1 = (bf16[128,2048]{1,0:T(8,128)(2,1)S(1)}, bf16[128,2048]{1,0:T(8,128)(2,1)}, u32[]{:S(2)}) copy-start(bf16[128,2048]{1,0:T(8,128)(2,1)} %param.10) | copy-start | bytes 1572868
Sparse Core Ops, SparseCore 0:
  9.8 22.9 all-gather.4
  95.3 55.4 all-reduce.3
  185.9 16.2 all-gather.10
  204.0 16.4 all-gather.8
  222.3 16.4 all-gather.6
  268.1 8.8 reduce-scatter.7
  290.4 8.8 reduce-scatter.3
  418.3 15.5 reduce-scatter.5
